TPU v7x, 256 devices: a whole 4x4x8 slice. The times are simulated.
256 devices in a mesh: gy: 4 (over x), gx: 4 (over z_hi), ga: 16 (over y, z_lo, core).
Axes of the slice: x: 4, y: 4, z: 8 (z_hi: 4, z_lo: 2; z = z_hi * 2 + z_lo), core: 2. Of those that a mesh axis runs over, the one named last changes fastest.
Arguments:
- volume: bfloat16 [16, 56, 56, 7, 768], P('ga', 'gy', 'gx'), may hold values from -6 to 6
- affinity: bfloat16 [16, 3, 56, 56, 7], P('ga', None, 'gy', 'gx'), may hold values from 0 to 1
- window_dest: int32 [16, 4, 4, 4], P('ga', 'gy', 'gx'), may hold values from 0 to 16, as said below
- qkv_weight: bfloat16 [768, 1152], replicated
- proj_weight: bfloat16 [384, 768], replicated, may hold values from -0.3125 to 0.3125
- head_weight: bfloat16 [768, 3], replicated, may hold values from -0.21875 to 0.21875
Outputs:
- grad_volume: bfloat16 [16, 56, 56, 7, 768], P('ga', 'gy', 'gx')
- grad_qkv: float32 [768, 1152], P('ga')
- grad_proj: float32 [384, 768], P(None, 'ga')
Inputs may be any that keep to these rules, and one draw needn't show every extreme that they name: `window_dest`: 16 marks an empty window; any other value names the device along ga, with the same gy and gx, that computes the window: the device itself or one of the min(2, 15) devices after it, cyclically (index plus 1, plus 2, modulo 16). Every device computes exactly 2 live windows, receives at most 1 from any one device, and in every group some device has 4 live windows (all of its windows), keeps 2 of them and sends 1 to each of the 2 devices after it along ga.
All inputs are finite; a program needn't handle non-finite values.
Results may differ from a plain program's by a relative error of at most 0.0065.
The roundings to bfloat16 on the way count: a program that leaves them out, or rounds other values in their place, can miss the bound.
Values may be sent and summed in bfloat16 or wider, within the bound.
No kernel may reach another device: no remote copies, remote signals or barrier semaphores. Data moves between devices by JAX's collectives and lax.ppermute only.
A program may use at most 128 MiB of HBM per device.

v0:
```python
import jax
import jax.numpy as jnp
from jax import lax
from jax.sharding import PartitionSpec as P

HEAD = 32
WIN = 7
HOPS = 2
LOSS_SCALE = 32.0
EPSILON = 1e-05


def passed_along(block, axis, distance):
    devices = range(lax.axis_size(axis))
    route = [((i - distance) % len(devices), i) for i in devices]
    return lax.ppermute(block, axis, route)


def for_sending(value):
    return jax.tree.map(lambda a: a.astype(jnp.bfloat16) if a.dtype == jnp.float32 else a, value)


def window_grads(tokens, target, region, qkv_weight, proj_weight, head_weight):
    inner_width = proj_weight.shape[0]
    head_count = inner_width // HEAD
    token_count = tokens.shape[0]
    score_scale = HEAD ** (-0.5)
    floated = tokens.astype(jnp.float32)
    mean_row = jnp.mean(floated, axis=-1, keepdims=True)
    centred = floated - mean_row
    variance = jnp.mean(centred * centred, axis=-1, keepdims=True)
    inv_std = lax.rsqrt(variance + EPSILON)
    unit_rows = centred * inv_std
    normed = unit_rows.astype(jnp.bfloat16)
    projected = jnp.dot(normed, qkv_weight, preferred_element_type=jnp.float32).astype(jnp.bfloat16)
    queries = projected[:, :inner_width].reshape(token_count, head_count, HEAD)
    key_rows = projected[:, inner_width : 2 * inner_width].reshape(token_count, head_count, HEAD)
    values = projected[:, 2 * inner_width :].reshape(token_count, head_count, HEAD)
    scores = (
        jnp.einsum("qhd,khd->hqk", queries, key_rows, preferred_element_type=jnp.float32)
        * score_scale
    )
    allowed = region[:, None] == region[None, :]
    scores = jnp.where(allowed[None], scores, jnp.float32(-1e30))
    row_max = jnp.max(scores, axis=-1, keepdims=True)
    exponent = jnp.exp(scores - row_max)
    attend = exponent / jnp.sum(exponent, axis=-1, keepdims=True)
    attend_low = attend.astype(jnp.bfloat16)
    mixed = (
        jnp.einsum("hqk,khd->qhd", attend_low, values, preferred_element_type=jnp.float32)
        .reshape(token_count, inner_width)
        .astype(jnp.bfloat16)
    )
    output = floated + jnp.dot(mixed, proj_weight, preferred_element_type=jnp.float32)
    output_low = output.astype(jnp.bfloat16)
    logits = jnp.dot(output_low, head_weight, preferred_element_type=jnp.float32)
    logit_grad = LOSS_SCALE * (jax.nn.sigmoid(logits) - target.T.astype(jnp.float32))
    output_grad = jnp.dot(
        logit_grad, head_weight.astype(jnp.float32).T, precision=lax.Precision.HIGHEST
    )
    grad_low = output_grad.astype(jnp.bfloat16)
    proj_term = jnp.dot(mixed.T, grad_low, preferred_element_type=jnp.float32)
    mixed_grad = jnp.dot(grad_low, proj_weight.T, preferred_element_type=jnp.float32).astype(
        jnp.bfloat16
    )
    mixed_grad = mixed_grad.reshape(token_count, head_count, HEAD)
    value_grad = jnp.einsum(
        "hqk,qhd->khd", attend_low, mixed_grad, preferred_element_type=jnp.float32
    )
    attend_grad = jnp.einsum("qhd,khd->hqk", mixed_grad, values, preferred_element_type=jnp.float32)
    score_grad = (
        attend * (attend_grad - jnp.sum(attend_grad * attend, axis=-1, keepdims=True)) * score_scale
    )
    score_low = score_grad.astype(jnp.bfloat16)
    query_grad = jnp.einsum("hqk,khd->qhd", score_low, key_rows, preferred_element_type=jnp.float32)
    key_grad = jnp.einsum("hqk,qhd->khd", score_low, queries, preferred_element_type=jnp.float32)
    qkv_grad = jnp.concatenate(
        [
            query_grad.reshape(token_count, inner_width),
            key_grad.reshape(token_count, inner_width),
            value_grad.reshape(token_count, inner_width),
        ],
        axis=1,
    ).astype(jnp.bfloat16)
    qkv_term = jnp.dot(normed.T, qkv_grad, preferred_element_type=jnp.float32)
    normed_grad = jnp.dot(qkv_grad, qkv_weight.T, preferred_element_type=jnp.float32)
    grad_mean = jnp.mean(normed_grad, axis=-1, keepdims=True)
    grad_along = jnp.mean(normed_grad * unit_rows, axis=-1, keepdims=True)
    cell_grad = output_grad + inv_std * (normed_grad - grad_mean - unit_rows * grad_along)
    return (cell_grad.astype(jnp.bfloat16), qkv_term, proj_term)


def to_windows(grid):
    cells_x, cells_y, cells_z = (grid.shape[0], grid.shape[1], grid.shape[2])
    trailing = grid.shape[3:]
    shaped = grid.reshape(
        (cells_x // WIN, WIN, cells_y // WIN, WIN, cells_z // WIN, WIN) + trailing
    )
    order = (0, 2, 4, 1, 3, 5) + tuple(range(6, 6 + len(trailing)))
    return shaped.transpose(order).reshape((-1, WIN**3) + trailing)


def from_windows(windows, cells_x, cells_y, cells_z):
    width = windows.shape[-1]
    shaped = windows.reshape(cells_x // WIN, cells_y // WIN, cells_z // WIN, WIN, WIN, WIN, width)
    return shaped.transpose(0, 3, 1, 4, 2, 5, 6).reshape(cells_x, cells_y, cells_z, width)


def region_grid(cells_x, cells_y, cells_z):
    margin = WIN // 2
    whole_x = cells_x * lax.axis_size("gy")
    whole_y = cells_y * lax.axis_size("gx")
    coord_x = lax.axis_index("gy") * cells_x + jnp.arange(cells_x, dtype=jnp.int32)
    coord_y = lax.axis_index("gx") * cells_y + jnp.arange(cells_y, dtype=jnp.int32)
    coord_z = jnp.arange(cells_z, dtype=jnp.int32)
    flag_x = (coord_x >= whole_x - margin).astype(jnp.int32)
    flag_y = (coord_y >= whole_y - margin).astype(jnp.int32)
    flag_z = (coord_z >= cells_z - margin).astype(jnp.int32)
    return flag_x[:, None, None] * 4 + flag_y[None, :, None] * 2 + flag_z[None, None, :]


def slot_select(wanted, count):
    rank = jnp.cumsum(wanted.astype(jnp.int32)) - 1
    chosen = wanted[None, :] & (rank[None, :] == jnp.arange(count, dtype=jnp.int32)[:, None])
    return chosen.astype(jnp.bfloat16)


def per_device(volume, affinity, window_dest, qkv_weight, proj_weight, head_weight):
    margin = WIN // 2
    cells_x, cells_y, cells_z, width = (
        volume.shape[1],
        volume.shape[2],
        volume.shape[3],
        volume.shape[4],
    )
    cells = WIN**3
    rim_first, rim_first_aff = passed_along((volume[:, :margin], affinity[:, :, :margin]), "gy", -1)
    grown = jnp.concatenate([volume[:, margin:], rim_first], axis=1)
    grown_aff = jnp.concatenate([affinity[:, :, margin:], rim_first_aff], axis=2)
    rim_second, rim_second_aff = passed_along(
        (grown[:, :, :margin], grown_aff[:, :, :, :margin]), "gx", -1
    )
    grown = jnp.concatenate([grown[:, :, margin:], rim_second], axis=2)
    grown_aff = jnp.concatenate([grown_aff[:, :, :, margin:], rim_second_aff], axis=3)
    grown = jnp.roll(grown[0], -margin, axis=2)
    grown_aff = jnp.roll(grown_aff[0], -margin, axis=3)
    tokens = to_windows(grown)
    targets = jnp.moveaxis(to_windows(jnp.moveaxis(grown_aff, 0, -1)), -1, 1)
    regions = to_windows(region_grid(cells_x, cells_y, cells_z))
    destinations = window_dest.reshape(-1)
    window_count = destinations.shape[0]
    group_size = lax.axis_size("ga")
    balance_count = window_count // 2
    zero_qkv = jnp.zeros(qkv_weight.shape, jnp.float32)
    zero_proj = jnp.zeros(proj_weight.shape, jnp.float32)

    def step(carry, item):
        cell_grad, qkv_term, proj_term = window_grads(
            item[0], item[1], item[2], qkv_weight, proj_weight, head_weight
        )
        return ((carry[0] + qkv_term, carry[1] + proj_term), cell_grad)

    slots = window_count // 4
    reach = min(HOPS, group_size - 1)
    own = lax.axis_index("ga")
    relative = jnp.where(destinations < group_size, (destinations - own) % group_size, -1)
    region_low = (regions + 1).astype(jnp.bfloat16)

    def pack(select_low):
        packed_tokens = jnp.einsum(
            "sw,wtd->std", select_low, tokens, preferred_element_type=jnp.float32
        ).astype(jnp.bfloat16)
        packed_targets = jnp.einsum(
            "sw,wat->sat", select_low, targets, preferred_element_type=jnp.float32
        ).astype(jnp.bfloat16)
        packed_regions = (
            jnp.einsum("sw,wt->st", select_low, region_low, preferred_element_type=jnp.float32)
            - 1.0
        ).astype(jnp.bfloat16)
        return (packed_tokens, packed_targets, packed_regions)

    kept_select = slot_select(relative == 0, balance_count)
    gathered = [pack(kept_select)]
    selects = []
    for offset in range(1, reach + 1):
        moved_select = slot_select(relative == offset, slots)
        selects.append(moved_select)
        gathered.append(passed_along(for_sending(pack(moved_select)), "ga", offset))
    got_tokens = jnp.concatenate([item[0] for item in gathered], axis=0)
    got_targets = jnp.concatenate([item[1] for item in gathered], axis=0)
    got_regions = jnp.concatenate([item[2] for item in gathered], axis=0)
    filled = got_regions[:, 0].astype(jnp.float32) >= 0.0
    filled_rank = jnp.cumsum(filled.astype(jnp.int32)) - 1
    pick = filled[None, :] & (
        filled_rank[None, :] == jnp.arange(balance_count, dtype=jnp.int32)[:, None]
    )
    pick_low = pick.astype(jnp.bfloat16)
    work_tokens = jnp.einsum(
        "bs,std->btd", pick_low, got_tokens, preferred_element_type=jnp.float32
    ).astype(jnp.bfloat16)
    work_targets = jnp.einsum(
        "bs,sat->bat", pick_low, got_targets, preferred_element_type=jnp.float32
    ).astype(jnp.bfloat16)
    work_regions = jnp.einsum(
        "bs,st->bt", pick_low, got_regions, preferred_element_type=jnp.float32
    ).astype(jnp.int32)
    (total_qkv, total_proj), work_grads = lax.scan(
        step, (zero_qkv, zero_proj), (work_tokens, work_targets, work_regions)
    )
    send_back = jnp.einsum(
        "bs,btd->std", pick_low, work_grads, preferred_element_type=jnp.float32
    ).astype(jnp.bfloat16)
    gathered_grad = jnp.einsum(
        "sw,std->wtd", kept_select, send_back[:balance_count], preferred_element_type=jnp.float32
    )
    for offset in range(1, reach + 1):
        begin = balance_count + (offset - 1) * slots
        returned = passed_along(send_back[begin : begin + slots], "ga", -offset)
        gathered_grad = gathered_grad + jnp.einsum(
            "sw,std->wtd", selects[offset - 1], returned, preferred_element_type=jnp.float32
        )
    window_grad = gathered_grad.astype(jnp.bfloat16)
    grid_grad = from_windows(window_grad, cells_x, cells_y, cells_z)
    grid_grad = jnp.roll(grid_grad, margin, axis=2)
    back_second = passed_along(grid_grad[:, cells_y - margin :], "gx", 1)
    grid_grad = jnp.concatenate([back_second, grid_grad[:, : cells_y - margin]], axis=1)
    back_first = passed_along(grid_grad[cells_x - margin :], "gy", 1)
    grid_grad = jnp.concatenate([back_first, grid_grad[: cells_x - margin]], axis=0)
    share_qkv, share_proj = (
        lax.psum_scatter(total_qkv, "ga", scatter_dimension=0, tiled=True),
        lax.psum_scatter(total_proj, "ga", scatter_dimension=1, tiled=True),
    )
    summed_qkv, summed_proj = lax.psum((share_qkv, share_proj), ("gy", "gx"))
    live_cells = lax.axis_size("gy") * lax.axis_size("gx") * group_size * balance_count * cells
    factor = float(live_cells) ** (-0.5)
    return (grid_grad[None], summed_qkv * factor, summed_proj * factor)


def solution(mesh):
    placed = (
        P("ga", "gy", "gx", None, None),
        P("ga", None, "gy", "gx", None),
        P("ga", "gy", "gx", None),
        P(),
        P(),
        P(),
    )
    return jax.shard_map(
        per_device,
        mesh=mesh,
        in_specs=placed,
        out_specs=(P("ga", "gy", "gx", None, None), P("ga", None), P(None, "ga")),
        check_vma=False,
    )
```

profile of v0, /device:TPU:2, one launch (start us, length us, event | category | flops | bytes accessed | tf_op | source)
XLA Modules:
  0.0 543.5 jit_solution(7793813690417377618)
XLA Ops:
  22.0 8.0 %collective-permute-done.6 = bf16[1,3,3,14,7]{3,4,2,1,0:T(8,128)(2,1)S(1)} collective-permute-done((bf16[1,3,3,14,7]{3,4,2,1,0:T(8,128)(2,1)S(1)}, bf16[1,3,3,14,7]{3,4,2,1,0:T(8,128)(2,1)S(1)}, u32[]{:S(2)}, u32[]{:S(2)}) %collective-permute-start.6) | collective-permute-done | bytes 1796 | tf_op jit(solution)/shard_map/ppermute | solution.py:16
  30.1 4.6 collective-permute-start.7
  34.8 4.4 collective-permute-done.7
  41.6 4.6 collective-permute-start.3
  48.6 18.0 %collective-permute-done.3 = bf16[1,14,3,7,768]{4,3,2,1,0:T(8,128)(2,1)S(1)} collective-permute-done((bf16[1,14,3,7,768]{4,3,2,1,0:T(8,128)(2,1)S(1)}, bf16[1,14,3,7,768]{4,3,2,1,0:T(8,128)(2,1)S(1)}, u32[]{:S(2)}, u32[]{:S(2)}) %collective-permute-start.3) | collective-permute-done | bytes 451616 | tf_op jit(solution)/shard_map/ppermute | solution.py:16
  80.6 12.6 %collective-permute-done.4 = bf16[1,343,768]{2,1,0:T(8,128)(2,1)S(1)} collective-permute-done((bf16[1,343,768]{2,1,0:T(8,128)(2,1)S(1)}, bf16[1,343,768]{2,1,0:T(8,128)(2,1)S(1)}, u32[]{:S(2)}, u32[]{:S(2)}) %collective-permute-start.4) | collective-permute-done | bytes 526880 | tf_op jit(solution)/shard_map/ppermute | solution.py:16
  99.9 119.4 %while.15 = (s32[]{:T(128)}, f32[768,1152]{1,0:T(8,128)}, f32[384,768]{1,0:T(8,128)S(1)}, bf16[2,343,768]{2,1,0:T(8,128)(2,1)}, bf16[2,343,768]{2,1,0:T(8,128)(2...) while((s32[]{:T(128)}, f32[768,1152]{1,0:T(8,128)}, ...), condition=%wide.region_12.13_spmd.clone, body=%wide.region_4.12_spmd.clone.sunk | while | flops 3029209600 | bytes 97110760 | solution.py:207
  104.6 6.1 %fusion.227 = (f32[12,343]{1,0:T(8,128)S(1)}, f32[12,343,343]{1,2,0:T(8,128)}) fusion(pred[343,343]{0,1:T(8,128)(4,1)S(1)} %broadcast_compare_fusion.4, bf16[343,12,32]{0,2,1:T(8,128)(2,1)S(1)} %bitcast.327, bf16[343,12,32]{0,2,1:T(8,128)(2,1)} %bitcast.329), kind=kOutput, calls=%fused_computation.202.clone.1 | convolution fusion | flops 96001928 | bytes 6308113 | tf_op jit(solution)/shard_map/while/body/eval_jaxpr/sub | solution.py:46
  120.8 5.0 fusion.232
  125.8 10.9 %fusion.234 = bf16[12,32,343]{2,1,0:T(8,128)(2,1)} fusion(bf16[343,12,32]{0,2,1:T(8,128)(2,1)} %bitcast.330, f32[12,343,343]{1,2,0:T(8,128)} %fusion.232, f32[12,343,343]{1,2,0:T(8,128)} %get-tuple-element.243, f32[12,343]{1,0:T(8,128)S(1)} %get-tuple-element.244), kind=kOutput, calls=%fused_computation.32.clone.1 | convolution fusion | flops 100373120 | bytes 11837616 | tf_op jit(solution)/shard_map/while/body/eval_jaxpr/hqk,khd->qhd/dot_general | solution.py:75
  136.7 11.0 %fusion.233 = bf16[12,32,343]{2,1,0:T(8,128)(2,1)} fusion(bf16[343,12,32]{0,2,1:T(8,128)(2,1)} %bitcast.328, f32[12,343,343]{1,2,0:T(8,128)} %fusion.232, f32[12,343,343]{1,2,0:T(8,128)} %get-tuple-element.243, f32[12,343]{1,0:T(8,128)S(1)} %get-tuple-element.244), kind=kOutput, calls=%fused_computation.33.clone.1 | convolution fusion | flops 100373120 | bytes 11837616 | tf_op jit(solution)/shard_map/while/body/eval_jaxpr/hqk,qhd->khd/dot_general | solution.py:76
  163.5 6.1 %fusion.227 = (f32[12,343]{1,0:T(8,128)S(1)}, f32[12,343,343]{1,2,0:T(8,128)}) fusion(pred[343,343]{0,1:T(8,128)(4,1)S(1)} %broadcast_compare_fusion.4, bf16[343,12,32]{0,2,1:T(8,128)(2,1)S(1)} %bitcast.327, bf16[343,12,32]{0,2,1:T(8,128)(2,1)} %bitcast.329), kind=kOutput, calls=%fused_computation.202.clone.1 | convolution fusion | flops 96001928 | bytes 6308113 | tf_op jit(solution)/shard_map/while/body/eval_jaxpr/sub | solution.py:46
  179.7 5.0 fusion.232
  184.7 10.9 %fusion.234 = bf16[12,32,343]{2,1,0:T(8,128)(2,1)} fusion(bf16[343,12,32]{0,2,1:T(8,128)(2,1)} %bitcast.330, f32[12,343,343]{1,2,0:T(8,128)} %fusion.232, f32[12,343,343]{1,2,0:T(8,128)} %get-tuple-element.243, f32[12,343]{1,0:T(8,128)S(1)} %get-tuple-element.244), kind=kOutput, calls=%fused_computation.32.clone.1 | convolution fusion | flops 100373120 | bytes 11837616 | tf_op jit(solution)/shard_map/while/body/eval_jaxpr/hqk,khd->qhd/dot_general | solution.py:75
  195.6 11.0 %fusion.233 = bf16[12,32,343]{2,1,0:T(8,128)(2,1)} fusion(bf16[343,12,32]{0,2,1:T(8,128)(2,1)} %bitcast.328, f32[12,343,343]{1,2,0:T(8,128)} %fusion.232, f32[12,343,343]{1,2,0:T(8,128)} %get-tuple-element.243, f32[12,343]{1,0:T(8,128)S(1)} %get-tuple-element.244), kind=kOutput, calls=%fused_computation.33.clone.1 | convolution fusion | flops 100373120 | bytes 11837616 | tf_op jit(solution)/shard_map/while/body/eval_jaxpr/hqk,qhd->khd/dot_general | solution.py:76
  213.0 5.4 %convolution_add_fusion.6 = f32[768,1152]{1,0:T(8,128)} fusion(f32[768,1152]{1,0:T(8,128)} %get-tuple-element.263, pred[]{:T(512)S(6)} %compare.25, bf16[343,384]{0,1:T(8,128)(2,1)} %bitcast.326, bf16[343,384]{0,1:T(8,128)(2,1)} %bitcast.323, bf16[343,384]{0,1:T(8,128)(2,1)} %bitcast.321, f32[343]{0:T(512)S(1)} %add_rsqrt_fusion.2, ...), kind=kOutput, calls=%fused_computation.8.clone.1 | convolution fusion | flops 612122880 | bytes 8400645 | tf_op jit(solution)/shard_map/while/body/eval_jaxpr/dot_general | solution.py:85
  226.8 5.7 %collective-permute-start.10 = (bf16[1,343,768]{2,1,0:T(8,128)(2,1)S(1)}, bf16[1,343,768]{2,1,0:T(8,128)(2,1)S(1)}, u32[]{:S(2)}, u32[]{:S(2)}) collective-permute-start(bf16[1,343,768]{2,1,0:T(8,128)(2,1)S(1)} %copy.74), channel_id=1, source_target_pairs={{1,0},{2,1},{3,2},{4,3},{5,4},{6,5},{7,6},{8,7},{9,8},{10,9},{11,1... | collective-permute-start | bytes 1580552 | tf_op jit(solution)/shard_map/ppermute | solution.py:16
  232.5 5.2 collective-permute-done.11
  237.8 9.8 %collective-permute-done.10 = bf16[1,343,768]{2,1,0:T(8,128)(2,1)S(1)} collective-permute-done((bf16[1,343,768]{2,1,0:T(8,128)(2,1)S(1)}, bf16[1,343,768]{2,1,0:T(8,128)(2,1)S(1)}, u32[]{:S(2)}, u32[]{:S(2)}) %collective-permute-start.10) | collective-permute-done | bytes 526880 | tf_op jit(solution)/shard_map/ppermute | solution.py:16
  247.6 4.5 add_convert_fusion
  260.3 26.7 %collective-permute-done.12 = bf16[14,3,7,768]{3,2,1,0:T(8,128)(2,1)S(1)} collective-permute-done((bf16[14,3,7,768]{3,2,1,0:T(8,128)(2,1)S(1)}, bf16[14,3,7,768]{3,2,1,0:T(8,128)(2,1)S(1)}, u32[]{:S(2)}, u32[]{:S(2)}) %collective-permute-start.12) | collective-permute-done | bytes 451616 | tf_op jit(solution)/shard_map/ppermute | solution.py:16
  288.8 11.0 %reduce-scatter.5.cloned.1.call-done = f32[384,48]{0,1:T(8,128)} async-done(((f32[384,768]{0,1:T(8,128)}), f32[384,48]{0,1:T(8,128)}) %reduce-scatter.5.cloned.1.call-update) | async-done | bytes 73744 | tf_op jit(solution)/shard_map/reduce_scatter | solution.py:231
  299.8 72.3 %reduce-scatter.3.cloned.1.call-done = f32[48,1152]{1,0:T(8,128)} async-done(((f32[768,1152]{1,0:T(8,128)}), f32[48,1152]{1,0:T(8,128)}) %reduce-scatter.3.cloned.1.call-update) | async-done | bytes 221200 | tf_op jit(solution)/shard_map/reduce_scatter | solution.py:230
  375.5 158.1 %all-reduce.3.cloned.1.call-done = (f32[48,1152]{1,0:T(8,128)}, f32[384,48]{0,1:T(8,128)}) async-done(((f32[48,1152]{1,0:T(8,128)}, f32[384,48]{0,1:T(8,128)}), (f32[48,1152]{1,0:T(8,128)}, f32[384,48]{0,1:T(8,128)})) %all-reduce.3.cloned.1.call-update) | async-done | bytes 294928 | tf_op jit(solution)/shard_map/psum | solution.py:233
  (221 shorter events, 111.1 us)
Async XLA Ops:
  7.2 292.6 %reduce-scatter.5.cloned.1.call-start = ((), (), s32[]{:S(2)}) async-start(), calls=%async_computation.3 | async-start | bytes 1253376 | tf_op jit(solution)/shard_map/reduce_scatter | solution.py:231
  10.1 66.0 %copy-start.13 = (s32[1,1,1,4]{3,2,1,0:T(1,128)}, s32[1,1,1,4]{3,2,1,0:T(1,128)S(1)}, u32[]{:S(2)}) copy-start(s32[1,1,1,4]{3,2,1,0:T(1,128)S(1)} %get-tuple-element.148) | copy-start | bytes 52
  10.6 11.0 %collective-permute-start = (bf16[1,343]{1,0:T(2,128)(2,1)S(1)}, bf16[1,343]{1,0:T(2,128)(2,1)S(1)}, u32[]{:S(2)}, u32[]{:S(2)}) collective-permute-start(bf16[1,343]{1,0:T(2,128)(2,1)S(1)} %convert_element_type.190), channel_id=1, source_target_pairs={{15,0},{0,1},{1,2},{2,3},{3,4},{4,5},{5,6},{6,7},{7,8},{8,9},{9,10... | collective-permute-start | bytes 2066 | tf_op jit(solution)/shard_map/ppermute | solution.py:16
  10.9 65.2 %copy-start.15 = (pred[4]{0:T(512)(128)(4,1)}, pred[4]{0:T(512)(128)(4,1)S(1)}, u32[]{:S(2)}) copy-start(pred[4]{0:T(512)(128)(4,1)S(1)} %fusion.100) | copy-start | bytes 16
  11.0 10.6 %collective-permute-start.1 = (bf16[1,343]{1,0:T(2,128)(2,1)S(1)}, bf16[1,343]{1,0:T(2,128)(2,1)S(1)}, u32[]{:S(2)}, u32[]{:S(2)}) collective-permute-start(bf16[1,343]{1,0:T(2,128)(2,1)S(1)} %convert_element_type.193), channel_id=1, source_target_pairs={{14,0},{15,1},{0,2},{1,3},{2,4},{3,5},{4,6},{5,7},{6,8},{7,9},{8,1... | collective-permute-start | bytes 2066 | tf_op jit(solution)/shard_map/ppermute | solution.py:16
  14.9 25.8 %collective-permute-start.2 = (bf16[1,3,14,7,768]{4,3,2,1,0:T(8,128)(2,1)}, bf16[1,3,14,7,768]{4,3,2,1,0:T(8,128)(2,1)}, u32[]{:S(2)}, u32[]{:S(2)}) collective-permute-start(bf16[1,3,14,7,768]{4,3,2,1,0:T(8,128)(2,1)} %slice.83), channel_id=1, source_target_pairs={{64,0},{128,64},{192,128},{0,192},{65,1},{129,65},{193,129},{1,193... | collective-permute-start | bytes 1354760 | tf_op jit(solution)/shard_map/ppermute | solution.py:16
  16.1 13.9 %collective-permute-start.6 = (bf16[1,3,3,14,7]{3,4,2,1,0:T(8,128)(2,1)S(1)}, bf16[1,3,3,14,7]{3,4,2,1,0:T(8,128)(2,1)S(1)}, u32[]{:S(2)}, u32[]{:S(2)}) collective-permute-start(bf16[1,3,3,14,7]{3,4,2,1,0:T(8,128)(2,1)S(1)} %slice.89), channel_id=1, source_target_pairs={{64,0},{128,64},{192,128},{0,192},{65,1},{129,65},{193,129},{1,193... | collective-permute-start | bytes 5300 | tf_op jit(solution)/shard_map/ppermute | solution.py:16
  19.7 59.6 %copy-start.18 = (pred[2,4]{1,0:T(4,128)(4,1)}, pred[2,4]{1,0:T(4,128)(4,1)S(1)}, u32[]{:S(2)}) copy-start(pred[2,4]{1,0:T(4,128)(4,1)S(1)} %compare_and_fusion.1) | copy-start | bytes 28
  21.9 73.6 %copy-start.20 = (pred[2,4]{1,0:T(4,128)(4,1)}, pred[2,4]{1,0:T(4,128)(4,1)S(1)}, u32[]{:S(2)}) copy-start(pred[2,4]{1,0:T(4,128)(4,1)S(1)} %compare_and_fusion) | copy-start | bytes 28
  30.1 9.2 %collective-permute-start.7 = (bf16[1,3,14,3,7]{3,4,2,1,0:T(8,128)(2,1)S(1)}, bf16[1,3,14,3,7]{3,4,2,1,0:T(8,128)(2,1)S(1)}, u32[]{:S(2)}, u32[]{:S(2)}) collective-permute-start(bf16[1,3,14,3,7]{3,4,2,1,0:T(8,128)(2,1)S(1)} %pad_maximum_fusion.13), channel_id=1, source_target_pairs={{16,0},{32,16},{48,32},{0,48},{17,1},{33,17},{49,33},{1,49},{18,2}... | collective-permute-start | bytes 5300 | tf_op jit(solution)/shard_map/ppermute | solution.py:16
  41.6 24.9 %collective-permute-start.3 = (bf16[1,14,3,7,768]{4,3,2,1,0:T(8,128)(2,1)S(1)}, bf16[1,14,3,7,768]{4,3,2,1,0:T(8,128)(2,1)S(1)}, u32[]{:S(2)}, u32[]{:S(2)}) collective-permute-start(bf16[1,14,3,7,768]{4,3,2,1,0:T(8,128)(2,1)S(1)} %pad_maximum_fusion.12), channel_id=1, source_target_pairs={{16,0},{32,16},{48,32},{0,48},{17,1},{33,17},{49,33},{1,49},{18,2}... | collective-permute-start | bytes 1354760 | tf_op jit(solution)/shard_map/ppermute | solution.py:16
  46.4 32.8 %collective-permute-start.8 = (bf16[1,3,343]{2,0,1:T(2,128)(2,1)S(1)}, bf16[1,3,343]{2,0,1:T(2,128)(2,1)S(1)}, u32[]{:S(2)}, u32[]{:S(2)}) collective-permute-start(bf16[1,3,343]{2,0,1:T(2,128)(2,1)S(1)} %copy.69), channel_id=1, source_target_pairs={{15,0},{0,1},{1,2},{2,3},{3,4},{4,5},{5,6},{6,7},{7,8},{8,9},{9,10... | collective-permute-start | bytes 6182 | tf_op jit(solution)/shard_map/ppermute | solution.py:16
  46.5 32.6 %collective-permute-start.9 = (bf16[1,3,343]{2,0,1:T(2,128)(2,1)S(1)}, bf16[1,3,343]{2,0,1:T(2,128)(2,1)S(1)}, u32[]{:S(2)}, u32[]{:S(2)}) collective-permute-start(bf16[1,3,343]{2,0,1:T(2,128)(2,1)S(1)} %copy.70), channel_id=1, source_target_pairs={{14,0},{15,1},{0,2},{1,3},{2,4},{3,5},{4,6},{5,7},{6,8},{7,9},{8,1... | collective-permute-start | bytes 6182 | tf_op jit(solution)/shard_map/ppermute | solution.py:16
  77.4 15.8 %collective-permute-start.4 = (bf16[1,343,768]{2,1,0:T(8,128)(2,1)S(1)}, bf16[1,343,768]{2,1,0:T(8,128)(2,1)S(1)}, u32[]{:S(2)}, u32[]{:S(2)}) collective-permute-start(bf16[1,343,768]{2,1,0:T(8,128)(2,1)S(1)} %copy.102), channel_id=1, source_target_pairs={{15,0},{0,1},{1,2},{2,3},{3,4},{4,5},{5,6},{6,7},{7,8},{8,9},{9,10... | collective-permute-start | bytes 1580552 | tf_op jit(solution)/shard_map/ppermute | solution.py:16
  77.6 17.1 %collective-permute-start.5 = (bf16[1,343,768]{2,1,0:T(8,128)(2,1)S(1)}, bf16[1,343,768]{2,1,0:T(8,128)(2,1)S(1)}, u32[]{:S(2)}, u32[]{:S(2)}) collective-permute-start(bf16[1,343,768]{2,1,0:T(8,128)(2,1)S(1)} %copy.103), channel_id=1, source_target_pairs={{14,0},{15,1},{0,2},{1,3},{2,4},{3,5},{4,6},{5,7},{6,8},{7,9},{8,1... | collective-permute-start | bytes 1580552 | tf_op jit(solution)/shard_map/ppermute | solution.py:16
  220.8 151.2 %reduce-scatter.3.cloned.1.call-start = ((), (), s32[]{:S(2)}) async-start(), calls=%async_computation.2 | async-start | bytes 3760128 | tf_op jit(solution)/shard_map/reduce_scatter | solution.py:230
  221.6 312.0 %all-reduce.3.cloned.1.call-start = ((), (), s32[]{:S(2)}) async-start(), calls=%async_computation.4 | async-start | bytes 589824 | tf_op jit(solution)/shard_map/psum | solution.py:233
  226.5 11.2 %collective-permute-start.11 = (bf16[1,343,768]{2,1,0:T(8,128)(2,1)S(1)}, bf16[1,343,768]{2,1,0:T(8,128)(2,1)S(1)}, u32[]{:S(2)}, u32[]{:S(2)}) collective-permute-start(bf16[1,343,768]{2,1,0:T(8,128)(2,1)S(1)} %copy.75), channel_id=1, source_target_pairs={{2,0},{3,1},{4,2},{5,3},{6,4},{7,5},{8,6},{9,7},{10,8},{11,9},{12,... | collective-permute-start | bytes 1580552 | tf_op jit(solution)/shard_map/ppermute | solution.py:16
  226.8 20.8 %copy-start.12 = (f32[4]{0:T(128)S(1)}, f32[4]{0:T(128)}, u32[]{:S(2)}) copy-start(f32[4]{0:T(128)} %get-tuple-element.147) | copy-start | bytes 52
  226.8 20.8 %copy-start.19 = (pred[2,4]{1,0:T(4,128)(4,1)S(1)}, pred[2,4]{1,0:T(4,128)(4,1)}, u32[]{:S(2)}) copy-start(pred[2,4]{1,0:T(4,128)(4,1)} %copy-done.18) | copy-start | bytes 28
  226.8 20.7 %collective-permute-start.10 = (bf16[1,343,768]{2,1,0:T(8,128)(2,1)S(1)}, bf16[1,343,768]{2,1,0:T(8,128)(2,1)S(1)}, u32[]{:S(2)}, u32[]{:S(2)}) collective-permute-start(bf16[1,343,768]{2,1,0:T(8,128)(2,1)S(1)} %copy.74), channel_id=1, source_target_pairs={{1,0},{2,1},{3,2},{4,3},{5,4},{6,5},{7,6},{8,7},{9,8},{10,9},{11,1... | collective-permute-start | bytes 1580552 | tf_op jit(solution)/shard_map/ppermute | solution.py:16
  257.8 29.4 %copy-start.1 = (bf16[14,14,4,768]{3,2,1,0:T(4,128)(2,1)}, bf16[14,14,4,768]{3,2,1,0:T(4,128)(2,1)S(1)}, u32[]{:S(2)}) copy-start(bf16[14,14,4,768]{3,2,1,0:T(4,128)(2,1)S(1)} %slice.121) | copy-start | bytes 3612676
  258.1 28.9 %collective-permute-start.12 = (bf16[14,3,7,768]{3,2,1,0:T(8,128)(2,1)S(1)}, bf16[14,3,7,768]{3,2,1,0:T(8,128)(2,1)S(1)}, u32[]{:S(2)}, u32[]{:S(2)}) collective-permute-start(bf16[14,3,7,768]{3,2,1,0:T(8,128)(2,1)S(1)} %pad_maximum_fusion.11), channel_id=1, source_target_pairs={{48,0},{0,16},{16,32},{32,48},{49,1},{1,17},{17,33},{33,49},{50,2}... | collective-permute-start | bytes 1354760 | tf_op jit(solution)/shard_map/ppermute | solution.py:16
  287.2 84.9 %collective-permute-start.13 = (bf16[3,14,7,768]{3,2,1,0:T(8,128)(2,1)S(1)}, bf16[3,14,7,768]{3,2,1,0:T(8,128)(2,1)S(1)}, u32[]{:S(2)}, u32[]{:S(2)}) collective-permute-start(bf16[3,14,7,768]{3,2,1,0:T(8,128)(2,1)S(1)} %pad_maximum_fusion.10), channel_id=1, source_target_pairs={{192,0},{0,64},{64,128},{128,192},{193,1},{1,65},{65,129},{129,193... | collective-permute-start | bytes 1354760 | tf_op jit(solution)/shard_map/ppermute | solution.py:16
  (24 other events, 86.7 us)
Sparse Core Ops, SparseCore 0:
  220.9 78.7 reduce-scatter.4
  302.3 69.7 reduce-scatter.2
  374.8 158.7 all-reduce.2
where the time goes:
time: 550 us; the launch traced here: 543 us
  waiting for transfers between devices  327 us (59%)
  matrix products  124 us (23%)
  local copies, waits for them, and re-layouts  30.1 us (5%)
  starting transfers between devices  26.7 us (5%)
  other arithmetic  19.4 us (4%)
  between operations  14.5 us (3%)
    psum x1, waiting for transfers between devices, per_device(): summed_qkv, summed_proj = lax.psum((share_qkv, share_proj), ('gy', 'gx'))  158 us
    ppermute x14, waiting for transfers between devices, passed_along(): return lax.ppermute(block, axis, route)  85.3 us
    reduce_scatter x1, waiting for transfers between devices, per_device(): lax.psum_scatter(total_qkv, 'ga', scatter_dimension=0, tiled=True)  72.3 us
    ppermute x14, starting transfers between devices, passed_along(): return lax.ppermute(block, axis, route)  26.6 us
    dot_general x2, matrix products, window_grads(): jnp.einsum('hqk,qhd->khd', score_low, queries, preferred_element_type=jnp...  21.9 us
    dot_general x2, matrix products, window_grads(): jnp.einsum('hqk,khd->qhd', score_low, key_rows, preferred_element_type=jn...  21.8 us
    sub x2, matrix products, window_grads(): exponent = jnp.exp(scores - row_max)  12.3 us
  transfers between devices with their start and end apart: 17, of which 11 were waited for; matrix products, arithmetic and copies ran while one was open for 8% of the time, Pallas kernels for 0%

commit v1 on v0

--- a/solution.py
+++ b/solution.py
@@ -230,7 +230,7 @@
         lax.psum_scatter(total_qkv, "ga", scatter_dimension=0, tiled=True),
         lax.psum_scatter(total_proj, "ga", scatter_dimension=1, tiled=True),
     )
-    summed_qkv, summed_proj = lax.psum((share_qkv, share_proj), ("gy", "gx"))
+    summed_qkv, summed_proj = lax.psum(lax.psum((share_qkv, share_proj), "gy"), "gx")
     live_cells = lax.axis_size("gy") * lax.axis_size("gx") * group_size * balance_count * cells
     factor = float(live_cells) ** (-0.5)
     return (grid_grad[None], summed_qkv * factor, summed_proj * factor)

time: 550 us -> 491 us (0.89)
  waiting for transfers between devices: 327 us -> 269 us
    psum x1 -> x2, waiting for transfers between devices: 158 us -> 100 us  [the longest x1 53.5 us: per_device(): lax.psum(lax.psum((share_qkv, share_proj), 'gy'), 'gx')]
  transfers between devices with their start and end apart: 17 -> 18, of which waited for: 11 -> 12; matrix products, arithmetic and copies ran while one was open for 8% -> 8% of each run, Pallas kernels for 0% -> 0%
where the time goes in v1:
time: 491 us; the launch traced here: 484 us
  waiting for transfers between devices  269 us (55%)
  matrix products  124 us (25%)
  local copies, waits for them, and re-layouts  30.1 us (6%)
  starting transfers between devices  26.7 us (5%)
  other arithmetic  19.1 us (4%)
  between operations  14.5 us (3%)
    ppermute x14, waiting for transfers between devices, passed_along(): return lax.ppermute(block, axis, route)  85.3 us
    reduce_scatter x1, waiting for transfers between devices, per_device(): lax.psum_scatter(total_qkv, 'ga', scatter_dimension=0, tiled=True)  72.3 us
    psum x1, waiting for transfers between devices, per_device(): lax.psum(lax.psum((share_qkv, share_proj), 'gy'), 'gx')  53.5 us
    psum x1, waiting for transfers between devices, per_device(): lax.psum((share_qkv, share_proj), 'gy')  46.8 us
    ppermute x14, starting transfers between devices, passed_along(): return lax.ppermute(block, axis, route)  26.5 us
    dot_general x2, matrix products, window_grads(): jnp.einsum('hqk,qhd->khd', score_low, queries, preferred_element_type=jnp...  21.9 us
    dot_general x2, matrix products, window_grads(): jnp.einsum('hqk,khd->qhd', score_low, key_rows, preferred_element_type=jn...  21.8 us
    sub x2, matrix products, window_grads(): exponent = jnp.exp(scores - row_max)  12.3 us
  transfers between devices with their start and end apart: 18, of which 12 were waited for; matrix products, arithmetic and copies ran while one was open for 8% of the time, Pallas kernels for 0%

profile of v1, /device:TPU:2, one launch (start us, length us, event | category | flops | bytes accessed | tf_op | source)
XLA Modules:
  0.0 484.5 jit_solution(4621568000613979231)
XLA Ops:
  22.0 8.0 %collective-permute-done.6 = bf16[1,3,3,14,7]{3,4,2,1,0:T(8,128)(2,1)S(1)} collective-permute-done((bf16[1,3,3,14,7]{3,4,2,1,0:T(8,128)(2,1)S(1)}, bf16[1,3,3,14,7]{3,4,2,1,0:T(8,128)(2,1)S(1)}, u32[]{:S(2)}, u32[]{:S(2)}) %collective-permute-start.6) | collective-permute-done | bytes 1796 | tf_op jit(solution)/shard_map/ppermute | solution.py:16
  30.1 4.6 collective-permute-start.7
  41.6 4.6 collective-permute-start.3
  48.6 18.0 %collective-permute-done.3 = bf16[1,14,3,7,768]{4,3,2,1,0:T(8,128)(2,1)S(1)} collective-permute-done((bf16[1,14,3,7,768]{4,3,2,1,0:T(8,128)(2,1)S(1)}, bf16[1,14,3,7,768]{4,3,2,1,0:T(8,128)(2,1)S(1)}, u32[]{:S(2)}, u32[]{:S(2)}) %collective-permute-start.3) | collective-permute-done | bytes 451616 | tf_op jit(solution)/shard_map/ppermute | solution.py:16
  80.6 12.6 %collective-permute-done.4 = bf16[1,343,768]{2,1,0:T(8,128)(2,1)S(1)} collective-permute-done((bf16[1,343,768]{2,1,0:T(8,128)(2,1)S(1)}, bf16[1,343,768]{2,1,0:T(8,128)(2,1)S(1)}, u32[]{:S(2)}, u32[]{:S(2)}) %collective-permute-start.4) | collective-permute-done | bytes 526880 | tf_op jit(solution)/shard_map/ppermute | solution.py:16
  99.9 119.4 %while.15 = (s32[]{:T(128)}, f32[768,1152]{1,0:T(8,128)}, f32[384,768]{1,0:T(8,128)S(1)}, bf16[2,343,768]{2,1,0:T(8,128)(2,1)}, bf16[2,343,768]{2,1,0:T(8,128)(2...) while((s32[]{:T(128)}, f32[768,1152]{1,0:T(8,128)}, ...), condition=%wide.region_12.13_spmd.clone, body=%wide.region_4.12_spmd.clone.sunk | while | flops 3029209600 | bytes 97110760 | solution.py:207
  104.6 6.1 %fusion.227 = (f32[12,343]{1,0:T(8,128)S(1)}, f32[12,343,343]{1,2,0:T(8,128)}) fusion(pred[343,343]{0,1:T(8,128)(4,1)S(1)} %broadcast_compare_fusion.4, bf16[343,12,32]{0,2,1:T(8,128)(2,1)S(1)} %bitcast.327, bf16[343,12,32]{0,2,1:T(8,128)(2,1)} %bitcast.329), kind=kOutput, calls=%fused_computation.202.clone.1 | convolution fusion | flops 96001928 | bytes 6308113 | tf_op jit(solution)/shard_map/while/body/eval_jaxpr/sub | solution.py:46
  120.8 5.0 %fusion.232 = f32[12,343,343]{1,2,0:T(8,128)} fusion(bf16[343,12,32]{0,2,1:T(8,128)(2,1)} %bitcast.312, bf16[343,12,32]{0,2,1:T(8,128)(2,1)} %bitcast.315), kind=kOutput, calls=%fused_computation.205.clone.1 | convolution fusion | flops 90354432 | bytes 6174000 | tf_op jit(solution)/shard_map/while/body/eval_jaxpr/qhd,khd->hqk/dot_general | solution.py:70
  125.8 10.9 %fusion.234 = bf16[12,32,343]{2,1,0:T(8,128)(2,1)} fusion(bf16[343,12,32]{0,2,1:T(8,128)(2,1)} %bitcast.330, f32[12,343,343]{1,2,0:T(8,128)} %fusion.232, f32[12,343,343]{1,2,0:T(8,128)} %get-tuple-element.245, f32[12,343]{1,0:T(8,128)S(1)} %get-tuple-element.246), kind=kOutput, calls=%fused_computation.32.clone.1 | convolution fusion | flops 100373120 | bytes 11837616 | tf_op jit(solution)/shard_map/while/body/eval_jaxpr/hqk,khd->qhd/dot_general | solution.py:75
  136.7 11.0 %fusion.233 = bf16[12,32,343]{2,1,0:T(8,128)(2,1)} fusion(bf16[343,12,32]{0,2,1:T(8,128)(2,1)} %bitcast.328, f32[12,343,343]{1,2,0:T(8,128)} %fusion.232, f32[12,343,343]{1,2,0:T(8,128)} %get-tuple-element.245, f32[12,343]{1,0:T(8,128)S(1)} %get-tuple-element.246), kind=kOutput, calls=%fused_computation.33.clone.1 | convolution fusion | flops 100373120 | bytes 11837616 | tf_op jit(solution)/shard_map/while/body/eval_jaxpr/hqk,qhd->khd/dot_general | solution.py:76
  163.5 6.1 %fusion.227 = (f32[12,343]{1,0:T(8,128)S(1)}, f32[12,343,343]{1,2,0:T(8,128)}) fusion(pred[343,343]{0,1:T(8,128)(4,1)S(1)} %broadcast_compare_fusion.4, bf16[343,12,32]{0,2,1:T(8,128)(2,1)S(1)} %bitcast.327, bf16[343,12,32]{0,2,1:T(8,128)(2,1)} %bitcast.329), kind=kOutput, calls=%fused_computation.202.clone.1 | convolution fusion | flops 96001928 | bytes 6308113 | tf_op jit(solution)/shard_map/while/body/eval_jaxpr/sub | solution.py:46
  179.7 5.0 %fusion.232 = f32[12,343,343]{1,2,0:T(8,128)} fusion(bf16[343,12,32]{0,2,1:T(8,128)(2,1)} %bitcast.312, bf16[343,12,32]{0,2,1:T(8,128)(2,1)} %bitcast.315), kind=kOutput, calls=%fused_computation.205.clone.1 | convolution fusion | flops 90354432 | bytes 6174000 | tf_op jit(solution)/shard_map/while/body/eval_jaxpr/qhd,khd->hqk/dot_general | solution.py:70
  184.7 10.9 %fusion.234 = bf16[12,32,343]{2,1,0:T(8,128)(2,1)} fusion(bf16[343,12,32]{0,2,1:T(8,128)(2,1)} %bitcast.330, f32[12,343,343]{1,2,0:T(8,128)} %fusion.232, f32[12,343,343]{1,2,0:T(8,128)} %get-tuple-element.245, f32[12,343]{1,0:T(8,128)S(1)} %get-tuple-element.246), kind=kOutput, calls=%fused_computation.32.clone.1 | convolution fusion | flops 100373120 | bytes 11837616 | tf_op jit(solution)/shard_map/while/body/eval_jaxpr/hqk,khd->qhd/dot_general | solution.py:75
  195.6 11.0 %fusion.233 = bf16[12,32,343]{2,1,0:T(8,128)(2,1)} fusion(bf16[343,12,32]{0,2,1:T(8,128)(2,1)} %bitcast.328, f32[12,343,343]{1,2,0:T(8,128)} %fusion.232, f32[12,343,343]{1,2,0:T(8,128)} %get-tuple-element.245, f32[12,343]{1,0:T(8,128)S(1)} %get-tuple-element.246), kind=kOutput, calls=%fused_computation.33.clone.1 | convolution fusion | flops 100373120 | bytes 11837616 | tf_op jit(solution)/shard_map/while/body/eval_jaxpr/hqk,qhd->khd/dot_general | solution.py:76
  213.0 5.4 %convolution_add_fusion.6 = f32[768,1152]{1,0:T(8,128)} fusion(f32[768,1152]{1,0:T(8,128)} %get-tuple-element.265, pred[]{:T(512)S(6)} %compare.25, bf16[343,384]{0,1:T(8,128)(2,1)} %bitcast.326, bf16[343,384]{0,1:T(8,128)(2,1)} %bitcast.323, bf16[343,384]{0,1:T(8,128)(2,1)} %bitcast.321, f32[343]{0:T(512)S(1)} %add_rsqrt_fusion.2, ...), kind=kOutput, calls=%fused_computation.8.clone.1 | convolution fusion | flops 612122880 | bytes 8400645 | tf_op jit(solution)/shard_map/while/body/eval_jaxpr/dot_general | solution.py:85
  226.7 5.7 %collective-permute-start.10 = (bf16[1,343,768]{2,1,0:T(8,128)(2,1)S(1)}, bf16[1,343,768]{2,1,0:T(8,128)(2,1)S(1)}, u32[]{:S(2)}, u32[]{:S(2)}) collective-permute-start(bf16[1,343,768]{2,1,0:T(8,128)(2,1)S(1)} %copy.74), channel_id=1, source_target_pairs={{1,0},{2,1},{3,2},{4,3},{5,4},{6,5},{7,6},{8,7},{9,8},{10,9},{11,1... | collective-permute-start | bytes 1580552 | tf_op jit(solution)/shard_map/ppermute | solution.py:16
  232.5 5.2 %collective-permute-done.11 = bf16[1,343,768]{2,1,0:T(8,128)(2,1)S(1)} collective-permute-done((bf16[1,343,768]{2,1,0:T(8,128)(2,1)S(1)}, bf16[1,343,768]{2,1,0:T(8,128)(2,1)S(1)}, u32[]{:S(2)}, u32[]{:S(2)}) %collective-permute-start.11) | collective-permute-done | bytes 526880 | tf_op jit(solution)/shard_map/ppermute | solution.py:16
  237.7 9.8 %collective-permute-done.10 = bf16[1,343,768]{2,1,0:T(8,128)(2,1)S(1)} collective-permute-done((bf16[1,343,768]{2,1,0:T(8,128)(2,1)S(1)}, bf16[1,343,768]{2,1,0:T(8,128)(2,1)S(1)}, u32[]{:S(2)}, u32[]{:S(2)}) %collective-permute-start.10) | collective-permute-done | bytes 526880 | tf_op jit(solution)/shard_map/ppermute | solution.py:16
  247.6 4.5 add_convert_fusion
  260.2 26.7 %collective-permute-done.12 = bf16[14,3,7,768]{3,2,1,0:T(8,128)(2,1)S(1)} collective-permute-done((bf16[14,3,7,768]{3,2,1,0:T(8,128)(2,1)S(1)}, bf16[14,3,7,768]{3,2,1,0:T(8,128)(2,1)S(1)}, u32[]{:S(2)}, u32[]{:S(2)}) %collective-permute-start.12) | collective-permute-done | bytes 451616 | tf_op jit(solution)/shard_map/ppermute | solution.py:16
  289.4 10.2 %reduce-scatter.5.cloned.1.call-done = f32[384,48]{0,1:T(8,128)} async-done(((f32[384,768]{0,1:T(8,128)}), f32[384,48]{0,1:T(8,128)}) %reduce-scatter.5.cloned.1.call-update) | async-done | bytes 73744 | tf_op jit(solution)/shard_map/reduce_scatter | solution.py:231
  299.6 72.3 %reduce-scatter.3.cloned.1.call-done = f32[48,1152]{1,0:T(8,128)} async-done(((f32[768,1152]{1,0:T(8,128)}), f32[48,1152]{1,0:T(8,128)}) %reduce-scatter.3.cloned.1.call-update) | async-done | bytes 221200 | tf_op jit(solution)/shard_map/reduce_scatter | solution.py:230
  372.0 46.8 %all-reduce.7.cloned.1.call-done = (f32[48,1152]{1,0:T(8,128)}, f32[384,48]{0,1:T(8,128)}) async-done(((f32[48,1152]{1,0:T(8,128)}, f32[384,48]{0,1:T(8,128)}), (f32[48,1152]{1,0:T(8,128)}, f32[384,48]{0,1:T(8,128)})) %all-reduce.7.cloned.1.call-update) | async-done | bytes 294928 | tf_op jit(solution)/shard_map/psum | solution.py:233
  421.1 53.5 %all-reduce.5.cloned.1.call-done = (f32[48,1152]{1,0:T(8,128)}, f32[384,48]{0,1:T(8,128)}) async-done(((f32[48,1152]{1,0:T(8,128)}, f32[384,48]{0,1:T(8,128)}), (f32[48,1152]{1,0:T(8,128)}, f32[384,48]{0,1:T(8,128)})) %all-reduce.5.cloned.1.call-update) | async-done | bytes 294928 | tf_op jit(solution)/shard_map/psum | solution.py:233
  (222 shorter events, 115.1 us)
Async XLA Ops:
  7.2 292.4 %reduce-scatter.5.cloned.1.call-start = ((), (), s32[]{:S(2)}) async-start(), calls=%async_computation.3 | async-start | bytes 1253376 | tf_op jit(solution)/shard_map/reduce_scatter | solution.py:231
  10.1 66.0 %copy-start.12 = (s32[1,1,1,4]{3,2,1,0:T(1,128)}, s32[1,1,1,4]{3,2,1,0:T(1,128)S(1)}, u32[]{:S(2)}) copy-start(s32[1,1,1,4]{3,2,1,0:T(1,128)S(1)} %get-tuple-element.150) | copy-start | bytes 52
  10.6 11.0 %collective-permute-start = (bf16[1,343]{1,0:T(2,128)(2,1)S(1)}, bf16[1,343]{1,0:T(2,128)(2,1)S(1)}, u32[]{:S(2)}, u32[]{:S(2)}) collective-permute-start(bf16[1,343]{1,0:T(2,128)(2,1)S(1)} %convert_element_type.190), channel_id=1, source_target_pairs={{15,0},{0,1},{1,2},{2,3},{3,4},{4,5},{5,6},{6,7},{7,8},{8,9},{9,10... | collective-permute-start | bytes 2066 | tf_op jit(solution)/shard_map/ppermute | solution.py:16
  10.9 65.2 %copy-start.14 = (pred[4]{0:T(512)(128)(4,1)}, pred[4]{0:T(512)(128)(4,1)S(1)}, u32[]{:S(2)}) copy-start(pred[4]{0:T(512)(128)(4,1)S(1)} %fusion.100) | copy-start | bytes 16
  11.0 10.6 %collective-permute-start.1 = (bf16[1,343]{1,0:T(2,128)(2,1)S(1)}, bf16[1,343]{1,0:T(2,128)(2,1)S(1)}, u32[]{:S(2)}, u32[]{:S(2)}) collective-permute-start(bf16[1,343]{1,0:T(2,128)(2,1)S(1)} %convert_element_type.193), channel_id=1, source_target_pairs={{14,0},{15,1},{0,2},{1,3},{2,4},{3,5},{4,6},{5,7},{6,8},{7,9},{8,1... | collective-permute-start | bytes 2066 | tf_op jit(solution)/shard_map/ppermute | solution.py:16
  14.9 25.8 %collective-permute-start.2 = (bf16[1,3,14,7,768]{4,3,2,1,0:T(8,128)(2,1)}, bf16[1,3,14,7,768]{4,3,2,1,0:T(8,128)(2,1)}, u32[]{:S(2)}, u32[]{:S(2)}) collective-permute-start(bf16[1,3,14,7,768]{4,3,2,1,0:T(8,128)(2,1)} %slice.83), channel_id=1, source_target_pairs={{64,0},{128,64},{192,128},{0,192},{65,1},{129,65},{193,129},{1,193... | collective-permute-start | bytes 1354760 | tf_op jit(solution)/shard_map/ppermute | solution.py:16
  16.1 13.9 %collective-permute-start.6 = (bf16[1,3,3,14,7]{3,4,2,1,0:T(8,128)(2,1)S(1)}, bf16[1,3,3,14,7]{3,4,2,1,0:T(8,128)(2,1)S(1)}, u32[]{:S(2)}, u32[]{:S(2)}) collective-permute-start(bf16[1,3,3,14,7]{3,4,2,1,0:T(8,128)(2,1)S(1)} %slice.89), channel_id=1, source_target_pairs={{64,0},{128,64},{192,128},{0,192},{65,1},{129,65},{193,129},{1,193... | collective-permute-start | bytes 5300 | tf_op jit(solution)/shard_map/ppermute | solution.py:16
  19.7 59.6 %copy-start.17 = (pred[2,4]{1,0:T(4,128)(4,1)}, pred[2,4]{1,0:T(4,128)(4,1)S(1)}, u32[]{:S(2)}) copy-start(pred[2,4]{1,0:T(4,128)(4,1)S(1)} %compare_and_fusion.1) | copy-start | bytes 28
  21.9 73.6 %copy-start.19 = (pred[2,4]{1,0:T(4,128)(4,1)}, pred[2,4]{1,0:T(4,128)(4,1)S(1)}, u32[]{:S(2)}) copy-start(pred[2,4]{1,0:T(4,128)(4,1)S(1)} %compare_and_fusion) | copy-start | bytes 28
  30.1 9.2 %collective-permute-start.7 = (bf16[1,3,14,3,7]{3,4,2,1,0:T(8,128)(2,1)S(1)}, bf16[1,3,14,3,7]{3,4,2,1,0:T(8,128)(2,1)S(1)}, u32[]{:S(2)}, u32[]{:S(2)}) collective-permute-start(bf16[1,3,14,3,7]{3,4,2,1,0:T(8,128)(2,1)S(1)} %pad_maximum_fusion.13), channel_id=1, source_target_pairs={{16,0},{32,16},{48,32},{0,48},{17,1},{33,17},{49,33},{1,49},{18,2}... | collective-permute-start | bytes 5300 | tf_op jit(solution)/shard_map/ppermute | solution.py:16
  41.6 24.9 %collective-permute-start.3 = (bf16[1,14,3,7,768]{4,3,2,1,0:T(8,128)(2,1)S(1)}, bf16[1,14,3,7,768]{4,3,2,1,0:T(8,128)(2,1)S(1)}, u32[]{:S(2)}, u32[]{:S(2)}) collective-permute-start(bf16[1,14,3,7,768]{4,3,2,1,0:T(8,128)(2,1)S(1)} %pad_maximum_fusion.12), channel_id=1, source_target_pairs={{16,0},{32,16},{48,32},{0,48},{17,1},{33,17},{49,33},{1,49},{18,2}... | collective-permute-start | bytes 1354760 | tf_op jit(solution)/shard_map/ppermute | solution.py:16
  46.4 32.8 %collective-permute-start.8 = (bf16[1,3,343]{2,0,1:T(2,128)(2,1)S(1)}, bf16[1,3,343]{2,0,1:T(2,128)(2,1)S(1)}, u32[]{:S(2)}, u32[]{:S(2)}) collective-permute-start(bf16[1,3,343]{2,0,1:T(2,128)(2,1)S(1)} %copy.69), channel_id=1, source_target_pairs={{15,0},{0,1},{1,2},{2,3},{3,4},{4,5},{5,6},{6,7},{7,8},{8,9},{9,10... | collective-permute-start | bytes 6182 | tf_op jit(solution)/shard_map/ppermute | solution.py:16
  46.5 32.6 %collective-permute-start.9 = (bf16[1,3,343]{2,0,1:T(2,128)(2,1)S(1)}, bf16[1,3,343]{2,0,1:T(2,128)(2,1)S(1)}, u32[]{:S(2)}, u32[]{:S(2)}) collective-permute-start(bf16[1,3,343]{2,0,1:T(2,128)(2,1)S(1)} %copy.70), channel_id=1, source_target_pairs={{14,0},{15,1},{0,2},{1,3},{2,4},{3,5},{4,6},{5,7},{6,8},{7,9},{8,1... | collective-permute-start | bytes 6182 | tf_op jit(solution)/shard_map/ppermute | solution.py:16
  77.4 15.8 %collective-permute-start.4 = (bf16[1,343,768]{2,1,0:T(8,128)(2,1)S(1)}, bf16[1,343,768]{2,1,0:T(8,128)(2,1)S(1)}, u32[]{:S(2)}, u32[]{:S(2)}) collective-permute-start(bf16[1,343,768]{2,1,0:T(8,128)(2,1)S(1)} %copy.102), channel_id=1, source_target_pairs={{15,0},{0,1},{1,2},{2,3},{3,4},{4,5},{5,6},{6,7},{7,8},{8,9},{9,10... | collective-permute-start | bytes 1580552 | tf_op jit(solution)/shard_map/ppermute | solution.py:16
  77.6 17.1 %collective-permute-start.5 = (bf16[1,343,768]{2,1,0:T(8,128)(2,1)S(1)}, bf16[1,343,768]{2,1,0:T(8,128)(2,1)S(1)}, u32[]{:S(2)}, u32[]{:S(2)}) collective-permute-start(bf16[1,343,768]{2,1,0:T(8,128)(2,1)S(1)} %copy.103), channel_id=1, source_target_pairs={{14,0},{15,1},{0,2},{1,3},{2,4},{3,5},{4,6},{5,7},{6,8},{7,9},{8,1... | collective-permute-start | bytes 1580552 | tf_op jit(solution)/shard_map/ppermute | solution.py:16
  220.8 151.1 %reduce-scatter.3.cloned.1.call-start = ((), (), s32[]{:S(2)}) async-start(), calls=%async_computation.2 | async-start | bytes 3760128 | tf_op jit(solution)/shard_map/reduce_scatter | solution.py:230
  221.5 197.2 %all-reduce.7.cloned.1.call-start = ((), (), s32[]{:S(2)}) async-start(), calls=%async_computation.5 | async-start | bytes 589824 | tf_op jit(solution)/shard_map/psum | solution.py:233
  226.5 11.2 %collective-permute-start.11 = (bf16[1,343,768]{2,1,0:T(8,128)(2,1)S(1)}, bf16[1,343,768]{2,1,0:T(8,128)(2,1)S(1)}, u32[]{:S(2)}, u32[]{:S(2)}) collective-permute-start(bf16[1,343,768]{2,1,0:T(8,128)(2,1)S(1)} %copy.75), channel_id=1, source_target_pairs={{2,0},{3,1},{4,2},{5,3},{6,4},{7,5},{8,6},{9,7},{10,8},{11,9},{12,... | collective-permute-start | bytes 1580552 | tf_op jit(solution)/shard_map/ppermute | solution.py:16
  226.7 20.8 %copy-start.11 = (f32[4]{0:T(128)S(1)}, f32[4]{0:T(128)}, u32[]{:S(2)}) copy-start(f32[4]{0:T(128)} %get-tuple-element.149) | copy-start | bytes 52
  226.7 20.8 %copy-start.18 = (pred[2,4]{1,0:T(4,128)(4,1)S(1)}, pred[2,4]{1,0:T(4,128)(4,1)}, u32[]{:S(2)}) copy-start(pred[2,4]{1,0:T(4,128)(4,1)} %copy-done.17) | copy-start | bytes 28
  226.7 20.7 %collective-permute-start.10 = (bf16[1,343,768]{2,1,0:T(8,128)(2,1)S(1)}, bf16[1,343,768]{2,1,0:T(8,128)(2,1)S(1)}, u32[]{:S(2)}, u32[]{:S(2)}) collective-permute-start(bf16[1,343,768]{2,1,0:T(8,128)(2,1)S(1)} %copy.74), channel_id=1, source_target_pairs={{1,0},{2,1},{3,2},{4,3},{5,4},{6,5},{7,6},{8,7},{9,8},{10,9},{11,1... | collective-permute-start | bytes 1580552 | tf_op jit(solution)/shard_map/ppermute | solution.py:16
  258.1 28.9 %collective-permute-start.12 = (bf16[14,3,7,768]{3,2,1,0:T(8,128)(2,1)S(1)}, bf16[14,3,7,768]{3,2,1,0:T(8,128)(2,1)S(1)}, u32[]{:S(2)}, u32[]{:S(2)}) collective-permute-start(bf16[14,3,7,768]{3,2,1,0:T(8,128)(2,1)S(1)} %pad_maximum_fusion.11), channel_id=1, source_target_pairs={{48,0},{0,16},{16,32},{32,48},{49,1},{1,17},{17,33},{33,49},{50,2}... | collective-permute-start | bytes 1354760 | tf_op jit(solution)/shard_map/ppermute | solution.py:16
  287.9 130.8 %collective-permute-start.13 = (bf16[3,14,7,768]{3,2,1,0:T(8,128)(2,1)}, bf16[3,14,7,768]{3,2,1,0:T(8,128)(2,1)S(1)}, u32[]{:S(2)}, u32[]{:S(2)}) collective-permute-start(bf16[3,14,7,768]{3,2,1,0:T(8,128)(2,1)} %pad_maximum_fusion.10), channel_id=1, source_target_pairs={{192,0},{0,64},{64,128},{128,192},{193,1},{1,65},{65,129},{129,193... | collective-permute-start | bytes 1354760 | tf_op jit(solution)/shard_map/ppermute | solution.py:16
  371.9 102.7 %all-reduce.5.cloned.1.call-start = ((), (), s32[]{:S(2)}) async-start(), calls=%async_computation.4 | async-start | bytes 589824 | tf_op jit(solution)/shard_map/psum | solution.py:233
  (24 other events, 86.7 us)
Sparse Core Ops, SparseCore 0:
  220.9 78.6 reduce-scatter.4
  302.2 69.6 reduce-scatter.2
  374.3 44.4 all-reduce.6
  421.3 53.2 all-reduce.4
